TPU v7x, 128 devices: a whole 4x4x4 slice. The times are simulated.
128 devices in a mesh: req: 32 (over y, x, core), mlp: 4 (over z).
Axes of the slice: x: 4, y: 4, z: 4, core: 2. Of those that a mesh axis runs over, the one named last changes fastest.
Arguments:
- states: bfloat16 [8192, 2560], P('req')
- attn_gain: float32 [2560], replicated, may hold values from 0.1 to 1.9
- query_matrix: bfloat16 [2560, 2048], P(None, 'mlp')
- key_matrix: bfloat16 [2560, 1024], P(None, 'mlp')
- value_matrix: bfloat16 [2560, 1024], P(None, 'mlp'), may hold values from -0.125 to 0.125
- query_gain: float32 [256], replicated
- key_gain: float32 [256], replicated
- out_weight: bfloat16 [2048, 2560], P('mlp'), may hold values from -0.125 to 0.125
- post_gain: float32 [2560], replicated, may hold values from 0.1 to 1.9
- ffw_gain: float32 [2560], replicated, may hold values from 0.1 to 1.9
- gate_weight: bfloat16 [2560, 10240], P(None, 'req'), may hold values from -0.125 to 0.125
- up_weight: bfloat16 [2560, 10240], P(None, 'req'), may hold values from -0.125 to 0.125
- down_weight: bfloat16 [10240, 2560], P('req'), may hold values from -0.0625 to 0.0625
- post_ffw_gain: float32 [2560], replicated, may hold values from 0.1 to 1.9
- prefix_key_cache: bfloat16 [32, 512, 1024], P('req', None, 'mlp')
- prefix_value_cache: bfloat16 [32, 512, 1024], P('req', None, 'mlp'), may hold values from -6 to 6
- segment: int32 [8192], P('req'), may hold values from 0 to 15, as said below
- prefix_id: int32 [8192], P('req'), may hold values from 0 to 31, as said below
- owner_map: int32 [32], replicated, may hold values from 0 to 31, each once
Outputs:
- layer_out: bfloat16 [8192, 2560], P(('req', 'mlp'))
Inputs may be any that keep to these rules, and one draw needn't show every extreme that they name: Within each block of 256 rows, equal segment values mark one request and occupy contiguous rows; requests hold 16 or 32 tokens. `prefix_id`: all tokens of one request name the same prefix group. In each block of 256 rows at most 32 rows name prefix groups of the same owner, and one prefix group is named by exactly 32 rows of every block.
All inputs are finite; a program needn't handle non-finite values.
Results may differ from a plain program's by a relative error of at most 0.017.
The roundings to bfloat16 on the way count: a program that leaves them out, or rounds other values in their place, can miss the bound.
Values may be sent and summed in bfloat16 or wider, within the bound.
A program may use at most 128 MiB of HBM per device.

v0:
```python
import jax
import jax.numpy as jnp
from jax import lax
from jax.sharding import PartitionSpec as P

CAP = 32
EPS = 1e-06


def normed(values_in, gain_vec):
    return (
        values_in
        * lax.rsqrt(jnp.mean(values_in * values_in, axis=-1, keepdims=True) + EPS)
        * gain_vec
    )


def local_attention(query_rows, key_rows, value_rows, segment_rows, score_scale):
    scores = (
        jnp.einsum("tgqd,sgd->gqts", query_rows, key_rows, preferred_element_type=jnp.float32)
        * score_scale
    )
    row_count = segment_rows.shape[0]
    token_position = jnp.arange(row_count, dtype=jnp.int32)
    allowed = (segment_rows[:, None] == segment_rows[None, :]) & (
        token_position[:, None] >= token_position[None, :]
    )
    scores = jnp.where(allowed, scores, -jnp.inf)
    row_max = jnp.max(scores, axis=-1, keepdims=True)
    powers = jnp.exp(scores - row_max)
    row_sum = jnp.sum(powers, axis=-1, keepdims=True)
    weights = (powers / row_sum).astype(jnp.bfloat16)
    mixed = jnp.einsum("gqts,sgd->tgqd", weights, value_rows, preferred_element_type=jnp.float32)
    log_total = jnp.transpose((row_max + jnp.log(row_sum))[..., 0], (2, 0, 1))
    return (mixed, log_total)


def prefix_partials(incoming, stored_keys, stored_values, score_scale):
    sources, slot_count, head_cols = incoming.shape
    kv_heads = stored_keys.shape[1]
    head_dim = stored_keys.shape[2]
    query_group_width = head_cols // (kv_heads * head_dim)
    query_rows = incoming.reshape(sources * slot_count, kv_heads, query_group_width, head_dim)
    scores = (
        jnp.einsum("rgqd,kgd->rgqk", query_rows, stored_keys, preferred_element_type=jnp.float32)
        * score_scale
    )
    row_max = jnp.max(scores, axis=-1, keepdims=True)
    powers = jnp.exp(scores - row_max)
    row_sum = jnp.sum(powers, axis=-1, keepdims=True)
    weights = (powers / row_sum).astype(jnp.bfloat16)
    mixed = jnp.einsum("rgqk,kgd->rgqd", weights, stored_values, preferred_element_type=jnp.float32)
    mixed = lax.optimization_barrier(mixed.astype(jnp.bfloat16)).astype(jnp.float32)
    log_total = row_max[..., 0] + jnp.log(row_sum[..., 0])
    return (
        mixed.reshape(sources, slot_count, head_cols),
        log_total.reshape(sources, slot_count, kv_heads * query_group_width),
    )


def body(
    states,
    attn_gain,
    query_matrix,
    key_matrix,
    value_matrix,
    query_gain,
    key_gain,
    out_weight,
    post_gain,
    ffw_gain,
    gate_weight,
    up_weight,
    down_weight,
    post_ffw_gain,
    prefix_key_cache,
    prefix_value_cache,
    segment,
    prefix_id,
    owner_map,
):
    row_count = states.shape[0]
    head_dim = query_gain.shape[0]
    kv_heads = key_matrix.shape[1] // head_dim
    head_cols = query_matrix.shape[1]
    query_group_width = head_cols // (kv_heads * head_dim)
    score_scale = head_dim ** (-0.5)
    req_count = lax.axis_size("req")
    mlp_count = lax.axis_size("mlp")
    mlp_index = lax.axis_index("mlp")
    quarter = row_count // mlp_count
    states_f = states.astype(jnp.float32)
    normalized_input = normed(states_f, attn_gain).astype(jnp.bfloat16)
    unnormed_queries = jnp.dot(
        normalized_input, query_matrix, preferred_element_type=jnp.float32
    ).reshape(row_count, kv_heads, query_group_width, head_dim)
    query_vectors = normed(unnormed_queries, query_gain).astype(jnp.bfloat16)
    unnormed_keys = jnp.dot(
        normalized_input, key_matrix, preferred_element_type=jnp.float32
    ).reshape(row_count, kv_heads, head_dim)
    key_vectors = normed(unnormed_keys, key_gain).astype(jnp.bfloat16)
    value_vectors = (
        jnp.dot(normalized_input, value_matrix, preferred_element_type=jnp.float32)
        .astype(jnp.bfloat16)
        .reshape(row_count, kv_heads, head_dim)
    )
    prefix_count = owner_map.shape[0]
    prefix_onehot = (
        prefix_id[:, None] == jnp.arange(prefix_count, dtype=jnp.int32)[None, :]
    ).astype(jnp.int32)
    target = jnp.sum(prefix_onehot * owner_map[None, :], axis=1)
    to_owner = (target[:, None] == jnp.arange(req_count, dtype=jnp.int32)[None, :]).astype(
        jnp.float32
    )
    token_position = jnp.arange(row_count, dtype=jnp.int32)
    earlier = (token_position[:, None] > token_position[None, :]).astype(jnp.float32)
    counts = jnp.dot(earlier, to_owner, precision=lax.Precision.HIGHEST)
    slot_index = jnp.sum(to_owner * counts, axis=1).astype(jnp.int32)
    place_row = target * CAP + slot_index
    placing = (place_row[None, :] == jnp.arange(req_count * CAP, dtype=jnp.int32)[:, None]).astype(
        jnp.bfloat16
    )
    outgoing = (
        jnp.dot(
            placing, query_vectors.reshape(row_count, head_cols), preferred_element_type=jnp.float32
        )
        .astype(jnp.bfloat16)
        .reshape(req_count, CAP, head_cols)
    )
    stored_keys = prefix_key_cache[0].reshape(-1, kv_heads, head_dim)
    stored_values = prefix_value_cache[0].reshape(-1, kv_heads, head_dim)
    suffix_output, suffix_log_sum = local_attention(
        query_vectors, key_vectors, value_vectors, segment, score_scale
    )
    mixed, log_total = prefix_partials(
        lax.all_to_all(outgoing, "req", split_axis=0, concat_axis=0, tiled=True),
        stored_keys,
        stored_values,
        score_scale,
    )
    back_out = lax.all_to_all(
        mixed.astype(jnp.bfloat16), "req", split_axis=0, concat_axis=0, tiled=True
    ).astype(mixed.dtype)
    back_lse = lax.all_to_all(
        log_total.astype(jnp.bfloat16), "req", split_axis=0, concat_axis=0, tiled=True
    ).astype(log_total.dtype)
    prefix_out = back_out.reshape(req_count * CAP, head_cols)[place_row].reshape(
        row_count, kv_heads, query_group_width, head_dim
    )
    prefix_lse = back_lse.reshape(req_count * CAP, kv_heads * query_group_width)[place_row].reshape(
        row_count, kv_heads, query_group_width
    )
    prefix_out, prefix_lse = (prefix_out, prefix_lse)
    blend = jax.nn.sigmoid(prefix_lse - suffix_log_sum)[..., None]
    attended = (
        (blend * prefix_out + (1.0 - blend) * suffix_output)
        .astype(jnp.bfloat16)
        .reshape(row_count, head_cols)
    )
    partial_value = jnp.dot(attended, out_weight, preferred_element_type=jnp.float32)
    full_sum = lax.psum(partial_value.astype(jnp.bfloat16), "mlp").astype(jnp.float32)
    summed = lax.dynamic_slice_in_dim(full_sum, mlp_index * quarter, quarter, 0)
    own_rows = lax.dynamic_slice_in_dim(states_f, mlp_index * quarter, quarter, 0)
    residual = own_rows + normed(summed, post_gain)
    ffw_in = normed(residual, ffw_gain).astype(jnp.bfloat16)
    piece = lax.all_gather(ffw_in, "req", axis=0, tiled=True)
    gate_proj = jnp.dot(piece, gate_weight, preferred_element_type=jnp.float32)
    up_proj = jnp.dot(piece, up_weight, preferred_element_type=jnp.float32)
    hidden = (jax.nn.gelu(gate_proj, approximate=True) * up_proj).astype(jnp.bfloat16)
    down_sum = lax.psum_scatter(
        jnp.dot(hidden, down_weight, preferred_element_type=jnp.float32).astype(jnp.bfloat16),
        "req",
        scatter_dimension=0,
        tiled=True,
    ).astype(jnp.float32)
    return (residual + normed(down_sum, post_ffw_gain)).astype(jnp.bfloat16)


def solution(mesh):
    return jax.shard_map(
        body,
        mesh=mesh,
        in_specs=(
            P("req", None),
            P(),
            P(None, "mlp"),
            P(None, "mlp"),
            P(None, "mlp"),
            P(),
            P(),
            P("mlp", None),
            P(),
            P(),
            P(None, "req"),
            P(None, "req"),
            P("req", None),
            P(),
            P("req", None, "mlp"),
            P("req", None, "mlp"),
            P("req"),
            P("req"),
            P(),
        ),
        out_specs=P(("req", "mlp"), None),
        check_vma=False,
    )
```

profile of v0, /device:TPU:0, one launch (start us, length us, event | category | flops | bytes accessed | tf_op | source)
XLA Modules:
  0.0 342.5 jit_solution(14212697419758735946)
XLA Ops:
  6.5 0.9 select_reduce_fusion
  7.5 0.2 fusion.29
  7.7 1.7 multiply_reduce_fusion
  9.4 0.7 broadcast_bitcast_fusion
  10.0 4.1 %fusion.66 = (f32[256,512]{1,0:T(8,128)}, f32[256,512]{1,0:T(8,128)}) fusion(bf16[2560,512]{1,0:T(8,128)(2,1)} %param.21, f32[2560]{0:T(1024)} %param.20, f32[256]{0:T(256)S(1)} %add_rsqrt_fusion.2, bf16[256,2560]{1,0:T(8,128)(2,1)} %param.19), kind=kOutput, calls=%fused_computation.108 | convolution fusion | flops 673841152 | bytes 4992000 | tf_op jit(solution)/shard_map/dot_general | solution.py:94
  14.1 1.4 mul.266
  15.5 0.3 reduce_sum.93
  15.9 0.3 mul.267
  16.3 1.2 multiply_convert_fusion.2
  17.4 1.5 convolution_convert_fusion.2
  18.9 7.5 %all-to-all-start = ((bf16[32,32,512]{2,1,0:T(8,128)(2,1)}), bf16[32,32,512]{2,1,0:T(8,128)(2,1)}, u32[]{:S(2)}, u32[]{:S(2)}) async-start(bf16[32,32,512]{2,1,0:T(8,128)(2,1)} %bitcast.130), calls=%async_computation | async-start | bytes 2097152 | tf_op jit(solution)/shard_map/all_to_all | solution.py:136
  26.5 0.1 fusion.47
  26.6 3.2 multiply_reduce_fusion.2
  29.8 13.9 %all-to-all-done = bf16[32,32,512]{2,1,0:T(8,128)(2,1)} async-done(((bf16[32,32,512]{2,1,0:T(8,128)(2,1)}), bf16[32,32,512]{2,1,0:T(8,128)(2,1)}, u32[]{:S(2)}, u32[]{:S(2)}) %all-to-all-start) | async-done | bytes 1048608 | tf_op jit(solution)/shard_map/all_to_all | solution.py:136
  43.8 2.2 reshape.279
  46.0 2.0 bitcast_reduce_fusion
  48.0 1.9 copy-done.1
  49.9 0.7 fusion.1
  50.6 0.1 convert_element_type.106
  50.7 0.6 copy.99
  51.3 3.8 %all-to-all-start.1 = ((bf16[32,32,2]{1,2,0:T(2,128)(2,1)}), bf16[32,32,2]{1,2,0:T(2,128)(2,1)S(1)}, u32[]{:S(2)}, u32[]{:S(2)}) async-start(bf16[32,32,2]{1,2,0:T(2,128)(2,1)} %copy.99), calls=%async_computation.1 | async-start | bytes 32768 | tf_op jit(solution)/shard_map/all_to_all | solution.py:144
  55.1 3.5 %fusion.16 = bf16[1024,1,2,256]{3,0,2,1:T(8,128)(2,1)S(1)} fusion(f32[1024,2]{0,1:T(2,128)S(1)} %fusion.1, f32[1024,2]{0,1:T(2,128)S(1)} %get-tuple-element.9, f32[1024,2,512]{0,2,1:T(8,128)} %copy-done.1, bf16[1,512,256]{2,1,0:T(8,128)(2,1)S(1)} %copy-done.8), kind=kOutput, calls=%fused_computation.26 | convolution fusion | flops 541589504 | bytes 5521408 | tf_op jit(solution)/shard_map/rgqk,kgd->rgqd/dot_general | solution.py:52
  58.6 2.1 copy.106
  60.7 2.6 convert_element_type.114
  63.3 7.5 %all-to-all-start.2 = ((bf16[32,32,512]{2,1,0:T(8,128)(2,1)}), bf16[32,32,512]{2,1,0:T(8,128)(2,1)}, u32[]{:S(2)}, u32[]{:S(2)}) async-start(bf16[32,32,512]{2,1,0:T(8,128)(2,1)} %convert_element_type.114), calls=%async_computation.2 | async-start | bytes 2097152 | tf_op jit(solution)/shard_map/all_to_all | solution.py:141
  70.8 0.2 all-reduce.2.cloned.1.call-start
  71.1 0.4 fusion.67
  71.5 0.1 fusion.40
  71.6 0.7 copy-done.2
  72.2 0.3 copy.114
  72.5 0.7 gather_fusion
  73.4 14.8 %all-to-all-done.2 = bf16[32,32,512]{2,1,0:T(8,128)(2,1)} async-done(((bf16[32,32,512]{2,1,0:T(8,128)(2,1)}), bf16[32,32,512]{2,1,0:T(8,128)(2,1)}, u32[]{:S(2)}, u32[]{:S(2)}) %all-to-all-start.2) | async-done | bytes 1048608 | tf_op jit(solution)/shard_map/all_to_all | solution.py:141
  88.1 2.9 bitcast_convert_fusion
  91.0 2.8 gather_fusion.1
  93.8 1.0 copy.107
  94.8 2.9 fusion.26
  97.7 1.9 convolution_convert_fusion.1
  99.7 3.2 convert_element_type.100
  102.9 43.6 %all-reduce.2.cloned.1.call-done = bf16[256,2560]{1,0:T(8,128)(2,1)} async-done(((bf16[256,2560]{1,0:T(8,128)(2,1)}), bf16[256,2560]{1,0:T(8,128)(2,1)}) %all-reduce.2.cloned.1.call-update) | async-done | bytes 1310736 | tf_op jit(solution)/shard_map/psum | solution.py:161
  146.5 1.1 fusion.34
  147.7 1.5 multiply_reduce_fusion.1
  149.2 2.1 multiply_convert_fusion.1
  151.4 58.3 %all-gather.2.cloned.1.call-done = bf16[2048,2560]{1,0:T(8,128)(2,1)} async-done(((bf16[64,2560]{1,0:T(8,128)(2,1)}), bf16[2048,2560]{1,0:T(8,128)(2,1)}) %all-gather.2.cloned.1.call-update) | async-done | bytes 10485776 | tf_op jit(solution)/shard_map/all_gather | solution.py:166
  209.7 9.5 %fusion.68 = f32[2048,320]{0,1:T(8,128)} fusion(bf16[2048,2560]{1,0:T(8,128)(2,1)} %all-gather.2.cloned.1.call-done, bf16[2560,320]{0,1:T(8,128)(2,1)} %param.29), kind=kOutput, calls=%fused_computation.110 | convolution fusion | flops 3355443200 | bytes 14745600 | tf_op jit(solution)/shard_map/dot_general | solution.py:167
  219.2 15.6 %convolution_convert_fusion = bf16[2048,2560]{1,0:T(8,128)(2,1)} fusion(bf16[320,2560]{1,0:T(8,128)(2,1)} %param.31, bf16[2048,2560]{1,0:T(8,128)(2,1)} %all-gather.2.cloned.1.call-done, bf16[2560,320]{0,1:T(8,128)(2,1)} %param.30, f32[2048,320]{0,1:T(8,128)} %fusion.68), kind=kOutput, calls=%fused_computation.2 | convolution fusion | flops 6722682880 | bytes 26869760 | tf_op jit(solution)/shard_map/dot_general | solution.py:171
  234.9 97.7 %reduce-scatter.2.cloned.1.call-done = bf16[64,2560]{1,0:T(8,128)(2,1)} async-done(((bf16[2048,2560]{1,0:T(8,128)(2,1)}), bf16[64,2560]{1,0:T(8,128)(2,1)}) %reduce-scatter.2.cloned.1.call-update) | async-done | bytes 327696 | tf_op jit(solution)/shard_map/reduce_scatter | solution.py:170
  332.5 1.1 fusion.35
  333.7 2.3 fusion.38
  (45 shorter events, 0.4 us)
Async XLA Ops:
  6.5 91.2 %copy-start = (bf16[512,2560]{1,0:T(8,128)(2,1)S(1)}, bf16[512,2560]{1,0:T(8,128)(2,1)}, u32[]{:S(2)}) copy-start(bf16[512,2560]{1,0:T(8,128)(2,1)} %param.26) | copy-start | bytes 7864324
  16.2 10.2 %copy-start.7 = (s32[256]{0:T(256)S(1)}, s32[256]{0:T(256)}, u32[]{:S(2)}) copy-start(s32[256]{0:T(256)} %param.35) | copy-start | bytes 3076
  16.3 10.3 %copy-start.9 = (f32[2560]{0:T(1024)S(1)}, f32[2560]{0:T(1024)}, u32[]{:S(2)}) copy-start(f32[2560]{0:T(1024)} %param.20) | copy-start | bytes 30724
  18.9 24.9 %all-to-all-start = ((bf16[32,32,512]{2,1,0:T(8,128)(2,1)}), bf16[32,32,512]{2,1,0:T(8,128)(2,1)}, u32[]{:S(2)}, u32[]{:S(2)}) async-start(bf16[32,32,512]{2,1,0:T(8,128)(2,1)} %bitcast.130), calls=%async_computation | async-start | bytes 2097152 | tf_op jit(solution)/shard_map/all_to_all | solution.py:136
  26.6 19.4 %copy-start.3 = (bf16[1,512,256]{2,1,0:T(8,128)(2,1)S(1)}, bf16[1,512,256]{2,1,0:T(8,128)(2,1)}, u32[]{:S(2)}) copy-start(bf16[1,512,256]{2,1,0:T(8,128)(2,1)} %param.33) | copy-start | bytes 786436
  48.0 1.9 copy-start.1
  48.0 7.1 %copy-start.8 = (bf16[1,512,256]{2,1,0:T(8,128)(2,1)S(1)}, bf16[1,512,256]{2,1,0:T(8,128)(2,1)}, u32[]{:S(2)}) copy-start(bf16[1,512,256]{2,1,0:T(8,128)(2,1)} %param.34) | copy-start | bytes 786436
  51.3 12.0 %all-to-all-start.1 = ((bf16[32,32,2]{1,2,0:T(2,128)(2,1)}), bf16[32,32,2]{1,2,0:T(2,128)(2,1)S(1)}, u32[]{:S(2)}, u32[]{:S(2)}) async-start(bf16[32,32,2]{1,2,0:T(2,128)(2,1)} %copy.99), calls=%async_computation.1 | async-start | bytes 32768 | tf_op jit(solution)/shard_map/all_to_all | solution.py:144
  60.7 10.3 %copy-start.11 = (f32[256]{0:T(256)S(1)}, f32[256]{0:T(256)}, u32[]{:S(2)}) copy-start(f32[256]{0:T(256)} %param.25) | copy-start | bytes 3076
  60.7 10.3 %copy-start.12 = (f32[256,256]{0,1:T(8,128)S(1)}, f32[256,256]{0,1:T(8,128)}, u32[]{:S(2)}) copy-start(f32[256,256]{0,1:T(8,128)} %get-tuple-element.12) | copy-start | bytes 786436
  63.3 24.8 %all-to-all-start.2 = ((bf16[32,32,512]{2,1,0:T(8,128)(2,1)}), bf16[32,32,512]{2,1,0:T(8,128)(2,1)}, u32[]{:S(2)}, u32[]{:S(2)}) async-start(bf16[32,32,512]{2,1,0:T(8,128)(2,1)} %convert_element_type.114), calls=%async_computation.2 | async-start | bytes 2097152 | tf_op jit(solution)/shard_map/all_to_all | solution.py:141
  70.8 75.7 %all-reduce.2.cloned.1.call-start = ((), (), s32[]{:S(2)}) async-start(), calls=%async_computation.4 | async-start | bytes 2621440 | tf_op jit(solution)/shard_map/psum | solution.py:161
  71.4 0.8 copy-start.2
  91.0 3.8 %copy-start.10 = (f32[2560]{0:T(1024)S(1)}, f32[2560]{0:T(1024)}, u32[]{:S(2)}) copy-start(f32[2560]{0:T(1024)} %param.20) | copy-start | bytes 30724
  99.6 48.0 %copy-start.4 = (f32[2560]{0:T(1024)S(1)}, f32[2560]{0:T(1024)}, u32[]{:S(2)}) copy-start(f32[2560]{0:T(1024)} %param.27) | copy-start | bytes 30724
  99.7 110.0 %all-gather.2.cloned.1.call-start = ((), (), s32[]{:S(2)}) async-start(), calls=%async_computation.5 | async-start | bytes 10813440 | tf_op jit(solution)/shard_map/all_gather | solution.py:166
  99.7 49.4 %copy-start.5 = (f32[2560]{0:T(1024)S(1)}, f32[2560]{0:T(1024)}, u32[]{:S(2)}) copy-start(f32[2560]{0:T(1024)} %param.28) | copy-start | bytes 30724
  151.3 181.2 %reduce-scatter.2.cloned.1.call-start = ((), (), s32[]{:S(2)}) async-start(), calls=%async_computation.6 | async-start | bytes 10813440 | tf_op jit(solution)/shard_map/reduce_scatter | solution.py:170
  234.8 98.9 %copy-start.6 = (f32[2560]{0:T(1024)S(1)}, f32[2560]{0:T(1024)}, u32[]{:S(2)}) copy-start(f32[2560]{0:T(1024)} %param.32) | copy-start | bytes 30724
Sparse Core Ops, SparseCore 0:
  99.8 46.6 all-reduce.1
  151.5 58.1 all-gather.1
  235.0 97.5 reduce-scatter.1
where the time goes:
time: 343 us
  waiting for transfers between devices  228 us (66%)
  matrix products  44.8 us (13%)
  other arithmetic  19.4 us (6%)
  starting transfers between devices  19.1 us (6%)
  local copies, waits for them, and re-layouts  17.5 us (5%)
  between operations  13.4 us (4%)
    reduce_scatter x1, waiting for transfers between devices, body(): lax.psum_scatter(jnp.dot(hidden, down_weight, preferred_element_type=jnp....  97.7 us
    all_gather x1, waiting for transfers between devices, body(): piece = lax.all_gather(ffw_in, 'req', axis=0, tiled=True)  58.3 us
    psum x1, waiting for transfers between devices, body(): lax.psum(partial_value.astype(jnp.bfloat16), 'mlp').astype(jnp.float32)  43.6 us
    dot_general x1, matrix products, body(): jnp.dot(hidden, down_weight, preferred_element_type=jnp.float32)  15.6 us
    all_to_all x1, waiting for transfers between devices, body(): lax.all_to_all(mixed.astype(jnp.bfloat16), 'req', split_axis=0, concat_ax...  14.8 us
    all_to_all x1, waiting for transfers between devices, body(): lax.all_to_all(outgoing, 'req', split_axis=0, concat_axis=0, tiled=True)  13.9 us
    dot_general x1, matrix products, body(): gate_proj = jnp.dot(piece, gate_weight, preferred_element_type=jnp.float32)  9.52 us
    all_to_all x1, starting transfers between devices, body(): lax.all_to_all(outgoing, 'req', split_axis=0, concat_axis=0, tiled=True)  7.53 us
  transfers between devices with their start and end apart: 6, of which 5 were waited for; matrix products, arithmetic and copies ran while one was open for 5% of the time, Pallas kernels for 0%

commit v1 on v0

--- a/solution.py
+++ b/solution.py
@@ -163,7 +163,9 @@
     own_rows = lax.dynamic_slice_in_dim(states_f, mlp_index * quarter, quarter, 0)
     residual = own_rows + normed(summed, post_gain)
     ffw_in = normed(residual, ffw_gain).astype(jnp.bfloat16)
-    piece = lax.all_gather(ffw_in, "req", axis=0, tiled=True)
+    piece = jnp.concatenate(
+        lax.all_to_all(jnp.stack([ffw_in] * lax.axis_size("req")), "req", 0, 0), axis=0
+    )
     gate_proj = jnp.dot(piece, gate_weight, preferred_element_type=jnp.float32)
     up_proj = jnp.dot(piece, up_weight, preferred_element_type=jnp.float32)
     hidden = (jax.nn.gelu(gate_proj, approximate=True) * up_proj).astype(jnp.bfloat16)

time: 343 us -> 411 us (1.20)
  blocking collectives: 0 us -> 126 us
  waiting for transfers between devices: 228 us -> 169 us
    all_to_all x0 -> x1, blocking collectives: none -> 126 us  [body(): lax.all_to_all(jnp.stack([ffw_in] * lax.axis_size('req')), 'req', 0, 0)]
    all_gather x1 -> x0, waiting for transfers between devices: 58.3 us -> none  [body(): piece = lax.all_gather(ffw_in, 'req', axis=0, tiled=True)]
  transfers between devices with their start and end apart: 6 -> 5, of which waited for: 5 -> 4; matrix products, arithmetic and copies ran while one was open for 5% -> 4% of each run, Pallas kernels for 0% -> 0%
where the time goes in v1:
time: 411 us; the launch traced here: 410 us
  waiting for transfers between devices  169 us (41%)
  blocking collectives  126 us (31%)
  matrix products  45 us (11%)
  other arithmetic  20.9 us (5%)
  starting transfers between devices  19.1 us (5%)
  local copies, waits for them, and re-layouts  16.8 us (4%)
  between operations  13.7 us (3%)
    all_to_all x1, blocking collectives, body(): lax.all_to_all(jnp.stack([ffw_in] * lax.axis_size('req')), 'req', 0, 0)  126 us
    reduce_scatter x1, waiting for transfers between devices, body(): lax.psum_scatter(jnp.dot(hidden, down_weight, preferred_element_type=jnp....  96.8 us
    psum x1, waiting for transfers between devices, body(): lax.psum(partial_value.astype(jnp.bfloat16), 'mlp').astype(jnp.float32)  43.6 us
    dot_general x1, matrix products, body(): jnp.dot(hidden, down_weight, preferred_element_type=jnp.float32)  15.6 us
    all_to_all x1, waiting for transfers between devices, body(): lax.all_to_all(mixed.astype(jnp.bfloat16), 'req', split_axis=0, concat_ax...  14.8 us
    all_to_all x1, waiting for transfers between devices, body(): lax.all_to_all(outgoing, 'req', split_axis=0, concat_axis=0, tiled=True)  13.9 us
  transfers between devices with their start and end apart: 5, of which 4 were waited for; matrix products, arithmetic and copies ran while one was open for 4% of the time, Pallas kernels for 0%

profile of v1, /device:TPU:0, one launch (start us, length us, event | category | flops | bytes accessed | tf_op | source)
XLA Modules:
  0.0 410.2 jit_solution(17970818340888499431)
XLA Ops:
  6.5 0.9 select_reduce_fusion
  7.5 0.2 fusion.29
  7.7 1.7 multiply_reduce_fusion
  9.4 0.7 broadcast_bitcast_fusion
  10.0 4.1 fusion.66
  14.1 1.4 mul.266
  15.5 0.3 reduce_sum.93
  15.9 0.3 mul.267
  16.3 1.2 multiply_convert_fusion.2
  17.4 1.5 convolution_convert_fusion.2
  18.9 7.5 %all-to-all-start = ((bf16[32,32,512]{2,1,0:T(8,128)(2,1)}), bf16[32,32,512]{2,1,0:T(8,128)(2,1)}, u32[]{:S(2)}, u32[]{:S(2)}) async-start(bf16[32,32,512]{2,1,0:T(8,128)(2,1)} %bitcast.131), calls=%async_computation | async-start | bytes 2097152 | tf_op jit(solution)/shard_map/all_to_all | solution.py:136
  26.5 0.1 fusion.47
  26.6 3.2 multiply_reduce_fusion.2
  29.8 13.9 %all-to-all-done = bf16[32,32,512]{2,1,0:T(8,128)(2,1)} async-done(((bf16[32,32,512]{2,1,0:T(8,128)(2,1)}), bf16[32,32,512]{2,1,0:T(8,128)(2,1)}, u32[]{:S(2)}, u32[]{:S(2)}) %all-to-all-start) | async-done | bytes 1048608 | tf_op jit(solution)/shard_map/all_to_all | solution.py:136
  43.8 2.1 reshape.284
  45.9 3.9 bitcast_reduce_fusion
  49.8 2.9 fusion.1
  52.8 0.1 convert_element_type.106
  52.9 0.6 copy.99
  53.5 3.8 all-to-all-start.1
  57.3 3.5 fusion.16
  60.8 2.1 copy.106
  62.9 2.6 convert_element_type.114
  65.5 7.5 %all-to-all-start.2 = ((bf16[32,32,512]{2,1,0:T(8,128)(2,1)}), bf16[32,32,512]{2,1,0:T(8,128)(2,1)}, u32[]{:S(2)}, u32[]{:S(2)}) async-start(bf16[32,32,512]{2,1,0:T(8,128)(2,1)} %convert_element_type.114), calls=%async_computation.2 | async-start | bytes 2097152 | tf_op jit(solution)/shard_map/all_to_all | solution.py:141
  73.0 0.2 all-reduce.2.cloned.1.call-start
  73.2 0.4 fusion.67
  73.6 0.1 fusion.40
  73.7 0.7 copy-done.2
  74.4 0.3 copy.114
  74.7 0.7 gather_fusion
  75.5 14.8 %all-to-all-done.2 = bf16[32,32,512]{2,1,0:T(8,128)(2,1)} async-done(((bf16[32,32,512]{2,1,0:T(8,128)(2,1)}), bf16[32,32,512]{2,1,0:T(8,128)(2,1)}, u32[]{:S(2)}, u32[]{:S(2)}) %all-to-all-start.2) | async-done | bytes 1048608 | tf_op jit(solution)/shard_map/all_to_all | solution.py:141
  90.3 2.9 bitcast_convert_fusion
  93.2 2.8 gather_fusion.1
  96.0 1.0 copy.107
  97.0 2.9 fusion.26
  99.9 1.9 convolution_convert_fusion.1
  101.9 3.2 convert_element_type.100
  105.0 43.6 %all-reduce.2.cloned.1.call-done = bf16[256,2560]{1,0:T(8,128)(2,1)} async-done(((bf16[256,2560]{1,0:T(8,128)(2,1)}), bf16[256,2560]{1,0:T(8,128)(2,1)}) %all-reduce.2.cloned.1.call-update) | async-done | bytes 1310736 | tf_op jit(solution)/shard_map/psum | solution.py:161
  148.7 1.1 fusion.34
  149.9 1.5 multiply_reduce_fusion.1
  151.4 1.4 multiply_convert_fusion.1
  152.8 1.2 stack.2
  154.0 125.6 %all_to_all.20 = bf16[32,64,2560]{2,1,0:T(8,128)(2,1)} all-to-all(bf16[32,64,2560]{2,1,0:T(8,128)(2,1)S(1)} %stack.2), channel_id=1, replica_groups=mesh['req'=32,'mlp'=4] {'req'}, dimensions={0} | all-to-all | bytes 20971520 | tf_op jit(solution)/shard_map/all_to_all | solution.py:167
  279.6 7.8 %fusion.68 = f32[2048,320]{0,1:T(8,128)} fusion(bf16[2048,2560]{1,0:T(8,128)(2,1)} %bitcast.31, bf16[2560,320]{0,1:T(8,128)(2,1)S(1)} %copy-done.8), kind=kOutput, calls=%fused_computation.110 | convolution fusion | flops 3355443200 | bytes 14745600 | tf_op jit(solution)/shard_map/dot_general | solution.py:169
  287.4 15.6 %convolution_convert_fusion = bf16[2048,2560]{1,0:T(8,128)(2,1)} fusion(bf16[320,2560]{1,0:T(8,128)(2,1)} %param.31, bf16[2048,2560]{1,0:T(8,128)(2,1)} %bitcast.31, bf16[2560,320]{0,1:T(8,128)(2,1)} %param.30, f32[2048,320]{0,1:T(8,128)} %fusion.68), kind=kOutput, calls=%fused_computation.2 | convolution fusion | flops 6722682880 | bytes 26869760 | tf_op jit(solution)/shard_map/dot_general | solution.py:173
  303.1 96.8 %reduce-scatter.2.cloned.1.call-done = bf16[64,2560]{1,0:T(8,128)(2,1)} async-done(((bf16[2048,2560]{1,0:T(8,128)(2,1)}), bf16[64,2560]{1,0:T(8,128)(2,1)}) %reduce-scatter.2.cloned.1.call-update) | async-done | bytes 327696 | tf_op jit(solution)/shard_map/reduce_scatter | solution.py:172
  399.9 1.1 fusion.35
  401.0 2.3 fusion.38
  (46 shorter events, 0.4 us)
Async XLA Ops:
  6.5 93.3 %copy-start = (bf16[512,2560]{1,0:T(8,128)(2,1)S(1)}, bf16[512,2560]{1,0:T(8,128)(2,1)}, u32[]{:S(2)}) copy-start(bf16[512,2560]{1,0:T(8,128)(2,1)} %param.26) | copy-start | bytes 7864324
  16.2 10.2 %copy-start.7 = (s32[256]{0:T(256)S(1)}, s32[256]{0:T(256)}, u32[]{:S(2)}) copy-start(s32[256]{0:T(256)} %param.35) | copy-start | bytes 3076
  16.3 10.3 %copy-start.10 = (f32[2560]{0:T(1024)S(1)}, f32[2560]{0:T(1024)}, u32[]{:S(2)}) copy-start(f32[2560]{0:T(1024)} %param.20) | copy-start | bytes 30724
  18.9 24.9 %all-to-all-start = ((bf16[32,32,512]{2,1,0:T(8,128)(2,1)}), bf16[32,32,512]{2,1,0:T(8,128)(2,1)}, u32[]{:S(2)}, u32[]{:S(2)}) async-start(bf16[32,32,512]{2,1,0:T(8,128)(2,1)} %bitcast.131), calls=%async_computation | async-start | bytes 2097152 | tf_op jit(solution)/shard_map/all_to_all | solution.py:136
  26.6 19.3 %copy-start.3 = (bf16[1,512,256]{2,1,0:T(8,128)(2,1)S(1)}, bf16[1,512,256]{2,1,0:T(8,128)(2,1)}, u32[]{:S(2)}) copy-start(bf16[1,512,256]{2,1,0:T(8,128)(2,1)} %param.33) | copy-start | bytes 786436
  49.8 7.4 %copy-start.9 = (bf16[1,512,256]{2,1,0:T(8,128)(2,1)S(1)}, bf16[1,512,256]{2,1,0:T(8,128)(2,1)}, u32[]{:S(2)}) copy-start(bf16[1,512,256]{2,1,0:T(8,128)(2,1)} %param.34) | copy-start | bytes 786436
  53.5 12.0 %all-to-all-start.1 = ((bf16[32,32,2]{1,2,0:T(2,128)(2,1)}), bf16[32,32,2]{1,2,0:T(2,128)(2,1)S(1)}, u32[]{:S(2)}, u32[]{:S(2)}) async-start(bf16[32,32,2]{1,2,0:T(2,128)(2,1)} %copy.99), calls=%async_computation.1 | async-start | bytes 32768 | tf_op jit(solution)/shard_map/all_to_all | solution.py:144
  62.9 10.3 %copy-start.12 = (f32[256]{0:T(256)S(1)}, f32[256]{0:T(256)}, u32[]{:S(2)}) copy-start(f32[256]{0:T(256)} %param.25) | copy-start | bytes 3076
  62.9 10.3 %copy-start.13 = (f32[256,256]{0,1:T(8,128)S(1)}, f32[256,256]{0,1:T(8,128)}, u32[]{:S(2)}) copy-start(f32[256,256]{0,1:T(8,128)} %get-tuple-element.12) | copy-start | bytes 786436
  65.5 24.8 %all-to-all-start.2 = ((bf16[32,32,512]{2,1,0:T(8,128)(2,1)}), bf16[32,32,512]{2,1,0:T(8,128)(2,1)}, u32[]{:S(2)}, u32[]{:S(2)}) async-start(bf16[32,32,512]{2,1,0:T(8,128)(2,1)} %convert_element_type.114), calls=%async_computation.2 | async-start | bytes 2097152 | tf_op jit(solution)/shard_map/all_to_all | solution.py:141
  73.0 75.7 %all-reduce.2.cloned.1.call-start = ((), (), s32[]{:S(2)}) async-start(), calls=%async_computation.5 | async-start | bytes 2621440 | tf_op jit(solution)/shard_map/psum | solution.py:161
  73.6 0.8 copy-start.2
  93.1 3.8 copy-start.11
  101.8 48.0 %copy-start.4 = (f32[2560]{0:T(1024)S(1)}, f32[2560]{0:T(1024)}, u32[]{:S(2)}) copy-start(f32[2560]{0:T(1024)} %param.27) | copy-start | bytes 30724
  101.8 298.1 %reduce-scatter.2.cloned.1.call-start = ((), (), s32[]{:S(2)}) async-start(), calls=%async_computation.6 | async-start | bytes 10813440 | tf_op jit(solution)/shard_map/reduce_scatter | solution.py:172
  101.9 49.5 %copy-start.5 = (f32[2560]{0:T(1024)S(1)}, f32[2560]{0:T(1024)}, u32[]{:S(2)}) copy-start(f32[2560]{0:T(1024)} %param.28) | copy-start | bytes 30724
  154.0 125.6 %copy-start.8 = (bf16[2560,320]{0,1:T(8,128)(2,1)S(1)}, bf16[2560,320]{0,1:T(8,128)(2,1)}, u32[]{:S(2)}) copy-start(bf16[2560,320]{0,1:T(8,128)(2,1)} %param.29) | copy-start | bytes 4915204
  303.0 98.0 %copy-start.6 = (f32[2560]{0:T(1024)S(1)}, f32[2560]{0:T(1024)}, u32[]{:S(2)}) copy-start(f32[2560]{0:T(1024)} %param.32) | copy-start | bytes 30724
  303.0 100.3 %copy-start.1 = (bf16[512,2560]{1,0:T(8,128)(2,1)S(1)}, bf16[512,2560]{1,0:T(8,128)(2,1)}, u32[]{:S(2)}) copy-start(bf16[512,2560]{1,0:T(8,128)(2,1)} %param.26) | copy-start | bytes 7864324
Sparse Core Ops, SparseCore 0:
  101.9 46.6 all-reduce.1
  303.2 96.6 reduce-scatter.1
